TPU v7x, 32 devices: a whole 2x2x4 slice. The times are simulated.
32 devices in a mesh: dp: 2 (over x), seq: 16 (over z, y, core).
Axes of the slice: x: 2, y: 2, z: 4, core: 2. Of those that a mesh axis runs over, the one named last changes fastest.
Arguments:
- queries: bfloat16 [4096, 1024], P(('dp', 'seq')), parts along dimension 0, may hold values from -6 to 6
- keys: bfloat16 [4096, 1024], P(('dp', 'seq')), parts along dimension 0, may hold values from -6 to 6
- values: bfloat16 [4096, 1024], P(('dp', 'seq')), parts along dimension 0, may hold values from -36 to 36
- feat_weight: bfloat16 [16, 64, 256], replicated, may hold values from -0.75 to 0.75
- norm_gain: bfloat16 [1024], replicated, may hold values from 0.25 to 1.75
- counts: int32 [32, 16], P('dp'), parts along dimension 0, may hold values from 4 to 12, as said below
- offsets: int32 [32, 16], P('dp'), parts along dimension 0, may hold values from 0 to 127, as said below
Outputs:
- mixed: bfloat16 [4096, 1024], P(('dp', 'seq')), parts along dimension 0
There are 2 independent parts, one for each index of `dp`. A program takes and returns all parts, laid end to end along the dimension named above; an argument that names none is the same for every part. Nothing has to cross between parts.
Inputs may be any that keep to these rules, and one draw needn't show every extreme that they name: Each row and each column of counts sums to 128; every loader sends 12 rows to exactly one device. For each device d the ranges from offsets[j, d] to offsets[j, d] + counts[j, d] - 1 over all loaders j tile 0 to 127.
All inputs are finite; a program needn't handle non-finite values.
Results may differ from a plain program's by a relative error of at most 0.0023.
Values may be sent and summed in bfloat16 or wider, within the bound.
A program may use at most 192 MiB of HBM per device.

v0:
```python
import jax
import jax.numpy as jnp
from jax import lax
from jax.sharding import PartitionSpec as P


def entering(shard, axis, combine, identity):
    length, index = (lax.axis_size(axis), lax.axis_index(axis))
    everything = lax.all_gather(shard.astype(jnp.bfloat16), axis)
    start = jnp.broadcast_to(jnp.asarray(identity, shard.dtype), shard.shape)

    def turn(k, before):
        reached = k < index
        new = combine(before, everything[k].astype(shard.dtype))
        return jnp.where(reached, new, before)

    return lax.fori_loop(0, length, turn, start)


def feature_map(rows, weight):
    projected = jnp.dot(rows, weight, preferred_element_type=jnp.float32)
    return (jax.nn.elu(projected) + 1.0).astype(jnp.bfloat16)


def add_states(earlier, later):
    return earlier + later


def per_device(queries, keys, values, feat_weight, norm_gain, counts, offsets):
    row_total = queries.shape[0]
    device_count = lax.axis_size("seq")
    base_slots = row_total // device_count
    capacity = base_slots + base_slots // 2
    head_count = feat_weight.shape[0]
    value_width = values.shape[1] // head_count
    my_index = lax.axis_index("seq")
    slot_ids = jnp.arange(capacity, dtype=jnp.int32)
    row_ids = jnp.arange(row_total, dtype=jnp.int32)
    device_ids = jnp.arange(device_count, dtype=jnp.int32)
    own_counts = lax.dynamic_index_in_dim(counts, my_index, 0, keepdims=False)
    own_starts = jnp.cumsum(own_counts) - own_counts
    send_rows = jnp.minimum(own_starts[:, None] + slot_ids[None, :], row_total - 1).reshape(-1)
    out_query = jnp.take(queries, send_rows, axis=0).reshape(device_count, capacity, head_count, -1)
    out_key = jnp.take(keys, send_rows, axis=0).reshape(device_count, capacity, head_count, -1)
    out_value = jnp.take(values, send_rows, axis=0).reshape(
        device_count, capacity, head_count, value_width
    )
    column_counts = lax.dynamic_index_in_dim(counts, my_index, 1, keepdims=False)
    column_offsets = lax.dynamic_index_in_dim(offsets, my_index, 1, keepdims=False)
    owner_hot = (
        (row_ids[:, None] >= column_offsets[None, :])
        & (row_ids[:, None] < (column_offsets + column_counts)[None, :])
    ).astype(jnp.int32)
    source = jnp.sum(owner_hot * device_ids[None, :], axis=1)
    begin = jnp.sum(owner_hot * column_offsets[None, :], axis=1)
    pick = source * capacity + row_ids - begin

    def unpack(block):
        flat = block.reshape(block.shape[0] * block.shape[1], block.shape[2], block.shape[3])
        return jnp.take(flat, pick, axis=0).transpose(1, 0, 2)

    arrived = (
        lax.all_to_all(out_query, "seq", split_axis=0, concat_axis=0, tiled=True),
        lax.all_to_all(out_key, "seq", split_axis=0, concat_axis=0, tiled=True),
        lax.all_to_all(out_value, "seq", split_axis=0, concat_axis=0, tiled=True),
    )
    query_heads = unpack(arrived[0])
    key_heads = unpack(arrived[1])
    value_heads = unpack(arrived[2])

    def key_section(pieces):
        key_head, value_head, weight = pieces
        phi_key = feature_map(key_head, weight)
        state = jnp.einsum("tf,tv->fv", phi_key, value_head, preferred_element_type=jnp.float32)
        return (phi_key, state)

    phi_keys, states = lax.map(key_section, (key_heads, value_heads, feat_weight))
    prefix = entering(states, "seq", add_states, jnp.zeros_like(states))
    causal = row_ids[:, None] >= row_ids[None, :]
    gains = norm_gain.reshape(head_count, value_width)

    def query_section(pieces):
        query_head, phi_key, value_head, weight, carried, gain = pieces
        phi_query = feature_map(query_head, weight)
        scores = jnp.einsum("sf,tf->st", phi_query, phi_key, preferred_element_type=jnp.float32)
        scores = jnp.where(causal, scores, 0.0)
        attended = jnp.dot(scores, value_head.astype(jnp.float32), precision=lax.Precision.HIGHEST)
        attended = attended + jnp.dot(
            phi_query.astype(jnp.float32), carried, precision=lax.Precision.HIGHEST
        )
        centre = jnp.mean(attended, axis=1, keepdims=True)
        centred = attended - centre
        spread_sq = jnp.mean(centred * centred, axis=1, keepdims=True)
        return (centred * lax.rsqrt(spread_sq + 1e-05) * gain.astype(jnp.float32)[None, :]).astype(
            jnp.bfloat16
        )

    normed = lax.map(
        query_section, (query_heads, phi_keys, value_heads, feat_weight, prefix, gains)
    )
    out_rows = normed.transpose(1, 0, 2).reshape(row_total, head_count * value_width)
    back_rows = jnp.minimum(column_offsets[:, None] + slot_ids[None, :], row_total - 1).reshape(-1)
    returning = jnp.take(out_rows, back_rows, axis=0).reshape(device_count, capacity, -1)
    returned = lax.all_to_all(returning, "seq", split_axis=0, concat_axis=0, tiled=True)
    target_hot = (
        (row_ids[:, None] >= own_starts[None, :])
        & (row_ids[:, None] < (own_starts + own_counts)[None, :])
    ).astype(jnp.int32)
    target = jnp.sum(target_hot * device_ids[None, :], axis=1)
    first_row = jnp.sum(target_hot * own_starts[None, :], axis=1)
    pick_back = target * capacity + row_ids - first_row
    return jnp.take(returned.reshape(device_count * capacity, -1), pick_back, axis=0)


def solution(mesh):
    in_specs = (
        P(("dp", "seq"), None),
        P(("dp", "seq"), None),
        P(("dp", "seq"), None),
        P(),
        P(),
        P("dp", None),
        P("dp", None),
    )
    out_specs = P(("dp", "seq"), None)
    return jax.shard_map(
        per_device, mesh=mesh, in_specs=in_specs, out_specs=out_specs, check_vma=False
    )
```

profile of v0, /device:TPU:0, one launch (start us, length us, event | category | flops | bytes accessed | tf_op | source)
XLA Modules:
  0.0 345.8 jit_solution(6576418406946475759)
XLA Ops:
  14.6 7.4 %all-to-all-start.1 = ((bf16[16,2,6144]{2,1,0:T(2,128)(2,1)}), bf16[16,2,6144]{2,1,0:T(2,128)(2,1)S(1)}, u32[]{:S(2)}, u32[]{:S(2)}) async-start(bf16[16,2,6144]{2,1,0:T(2,128)(2,1)} %reshape.241), calls=%async_computation.1 | async-start | bytes 786432 | tf_op jit(solution)/shard_map/all_to_all | solution.py:64
  23.8 10.4 %all-to-all-done.1 = bf16[16,2,6144]{2,1,0:T(2,128)(2,1)S(1)} async-done(((bf16[16,2,6144]{2,1,0:T(2,128)(2,1)}), bf16[16,2,6144]{2,1,0:T(2,128)(2,1)S(1)}, u32[]{:S(2)}, u32[]{:S(2)}) %all-to-all-start.1) | async-done | bytes 393248 | tf_op jit(solution)/shard_map/all_to_all | solution.py:64
  34.1 3.6 %all-to-all-start.2 = ((bf16[16,2,6144]{2,1,0:T(2,128)(2,1)}), bf16[16,2,6144]{2,1,0:T(2,128)(2,1)S(1)}, u32[]{:S(2)}, u32[]{:S(2)}) async-start(bf16[16,2,6144]{2,1,0:T(2,128)(2,1)} %reshape.243), calls=%async_computation.2 | async-start | bytes 786432 | tf_op jit(solution)/shard_map/all_to_all | solution.py:65
  39.5 10.3 %all-to-all-done.2 = bf16[16,2,6144]{2,1,0:T(2,128)(2,1)S(1)} async-done(((bf16[16,2,6144]{2,1,0:T(2,128)(2,1)}), bf16[16,2,6144]{2,1,0:T(2,128)(2,1)S(1)}, u32[]{:S(2)}, u32[]{:S(2)}) %all-to-all-start.2) | async-done | bytes 393248 | tf_op jit(solution)/shard_map/all_to_all | solution.py:65
  49.8 3.6 %all-to-all-start = ((bf16[16,2,6144]{2,1,0:T(2,128)(2,1)}), bf16[16,2,6144]{2,1,0:T(2,128)(2,1)S(1)}, u32[]{:S(2)}, u32[]{:S(2)}) async-start(bf16[16,2,6144]{2,1,0:T(2,128)(2,1)} %reshape.239), calls=%async_computation | async-start | bytes 786432 | tf_op jit(solution)/shard_map/all_to_all | solution.py:63
  56.2 9.3 %all-to-all-done = bf16[16,2,6144]{2,1,0:T(2,128)(2,1)S(1)} async-done(((bf16[16,2,6144]{2,1,0:T(2,128)(2,1)}), bf16[16,2,6144]{2,1,0:T(2,128)(2,1)S(1)}, u32[]{:S(2)}, u32[]{:S(2)}) %all-to-all-start) | async-done | bytes 393248 | tf_op jit(solution)/shard_map/all_to_all | solution.py:63
  67.3 37.8 %while.37 = (s32[]{:T(128)}, bf16[16,128,256]{2,1,0:T(8,128)(2,1)}, bf16[16,256,64]{1,2,0:T(8,128)(2,1)}, bf16[16,128,64]{2,1,0:T(8,128)(2,1)S(1)}, bf16[16,64,2...) while((s32[]{:T(128)}, bf16[16,128,256]{2,1,0:T(8,128)(2,1)}, ...), condition=%wide.region_6.9_spmd, body=%wide.region_5.8_spmd.sunk | while | flops 8552450 | bytes 363085 | solution.py:77
  67.3 1.6 bitcast_dynamic-update-slice_fusion.2
  90.9 1.6 bitcast_dynamic-update-slice_fusion.2
  95.6 1.6 bitcast_dynamic-update-slice_fusion.2
  98.0 1.6 bitcast_dynamic-update-slice_fusion.2
  106.9 71.4 %all-gather.3.cloned.1.call-done = bf16[256,256,64]{1,2,0:T(8,128)(2,1)} async-done(((bf16[16,256,64]{1,2,0:T(8,128)(2,1)}), bf16[256,256,64]{1,2,0:T(8,128)(2,1)}) %all-gather.3.cloned.1.call-update) | async-done | bytes 8388624 | tf_op jit(solution)/shard_map/all_gather | solution.py:9
  178.3 73.9 %while.39 = (s32[]{:T(128)}, f32[16,256,64]{2,1,0:T(8,128)S(1)}, s32[]{:T(128)}, bf16[16,16,256,64]{2,3,1,0:T(8,128)(2,1)}, s32[]{:T(128)}, /*index=5*/s32[]{:T(128)}) while((s32[]{:T(128)}, f32[16,256,64]{2,1,0:T(8,128)S(1)}, s32[]{:T(128)}, bf16[16,16,256,64]{2,3,1,0:T(8,128)(2,1)}, s32[]{:T(128)}, /*index=5*/s32[]{:T(128)}) %tuple.98), condition=%wide.region_8.11_spmd.clone, body=%wide.region_7.10_spmd.clone.sunk | while | flops 1048580 | bytes 4718685 | solution.py:17
  178.3 1.9 constant_dynamic-slice_fusion.4
  182.9 1.9 constant_dynamic-slice_fusion.4
  187.5 1.9 constant_dynamic-slice_fusion.4
  192.1 1.9 constant_dynamic-slice_fusion.4
  196.7 1.9 constant_dynamic-slice_fusion.4
  201.4 1.9 constant_dynamic-slice_fusion.4
  206.0 1.9 constant_dynamic-slice_fusion.4
  210.6 1.9 constant_dynamic-slice_fusion.4
  215.2 1.9 constant_dynamic-slice_fusion.4
  219.8 1.9 constant_dynamic-slice_fusion.4
  224.5 1.9 constant_dynamic-slice_fusion.4
  229.1 1.9 constant_dynamic-slice_fusion.4
  233.7 1.9 constant_dynamic-slice_fusion.4
  238.3 1.9 constant_dynamic-slice_fusion.4
  242.9 1.9 constant_dynamic-slice_fusion.4
  247.5 1.9 constant_dynamic-slice_fusion.4
  252.2 64.2 %while.38 = (s32[]{:T(128)}, bf16[16,128,64]{1,2,0:T(8,128)(2,1)}, bf16[16,128,64]{2,1,0:T(8,128)(2,1)}, bf16[16,64,256]{2,1,0:T(8,128)(2,1)}, bf16[16,128,256]{...) while((s32[]{:T(128)}, bf16[16,128,64]{1,2,0:T(8,128)(2,1)}, ...), condition=%wide.region_12.15_spmd.clone, body=%wide.region_9.14_spmd.clone.sunk | while | flops 50602176 | bytes 810725 | solution.py:98
  319.4 3.6 %all-to-all-start.3 = ((bf16[16,12,1024]{2,1,0:T(8,128)(2,1)}), bf16[16,12,1024]{2,1,0:T(8,128)(2,1)S(1)}, u32[]{:S(2)}, u32[]{:S(2)}) async-start(bf16[16,12,1024]{2,1,0:T(8,128)(2,1)} %reshape.143), calls=%async_computation.3 | async-start | bytes 1048576 | tf_op jit(solution)/shard_map/all_to_all | solution.py:104
  323.1 14.1 %all-to-all-done.3 = bf16[16,12,1024]{2,1,0:T(8,128)(2,1)S(1)} async-done(((bf16[16,12,1024]{2,1,0:T(8,128)(2,1)}), bf16[16,12,1024]{2,1,0:T(8,128)(2,1)S(1)}, u32[]{:S(2)}, u32[]{:S(2)}) %all-to-all-start.3) | async-done | bytes 393248 | tf_op jit(solution)/shard_map/all_to_all | solution.py:104
  (274 shorter events, 160.5 us)
Async XLA Ops:
  6.5 3.0 copy-start
  6.5 4.0 %copy-start.1 = (bf16[128,1024]{1,0:T(8,128)(2,1)S(1)}, bf16[128,1024]{1,0:T(8,128)(2,1)}, u32[]{:S(2)}) copy-start(bf16[128,1024]{1,0:T(8,128)(2,1)} %param.19) | copy-start | bytes 786436
  10.5 1.0 copy-start.2
  14.6 19.6 %all-to-all-start.1 = ((bf16[16,2,6144]{2,1,0:T(2,128)(2,1)}), bf16[16,2,6144]{2,1,0:T(2,128)(2,1)S(1)}, u32[]{:S(2)}, u32[]{:S(2)}) async-start(bf16[16,2,6144]{2,1,0:T(2,128)(2,1)} %reshape.241), calls=%async_computation.1 | async-start | bytes 786432 | tf_op jit(solution)/shard_map/all_to_all | solution.py:64
  23.8 29.7 %copy-start.4 = (s32[16,16]{1,0:T(8,128)S(1)}, s32[16,16]{1,0:T(8,128)}, u32[]{:S(2)}) copy-start(s32[16,16]{1,0:T(8,128)} %param.22) | copy-start | bytes 3076
  34.1 15.7 %all-to-all-start.2 = ((bf16[16,2,6144]{2,1,0:T(2,128)(2,1)}), bf16[16,2,6144]{2,1,0:T(2,128)(2,1)S(1)}, u32[]{:S(2)}, u32[]{:S(2)}) async-start(bf16[16,2,6144]{2,1,0:T(2,128)(2,1)} %reshape.243), calls=%async_computation.2 | async-start | bytes 786432 | tf_op jit(solution)/shard_map/all_to_all | solution.py:65
  49.8 15.7 %all-to-all-start = ((bf16[16,2,6144]{2,1,0:T(2,128)(2,1)}), bf16[16,2,6144]{2,1,0:T(2,128)(2,1)S(1)}, u32[]{:S(2)}, u32[]{:S(2)}) async-start(bf16[16,2,6144]{2,1,0:T(2,128)(2,1)} %reshape.239), calls=%async_computation | async-start | bytes 786432 | tf_op jit(solution)/shard_map/all_to_all | solution.py:63
  53.4 124.9 %all-gather.3.cloned.1.call-start = ((), (), s32[]{:S(2)}) async-start(), calls=%async_computation.4 | async-start | bytes 8912896 | tf_op jit(solution)/shard_map/all_gather | solution.py:9
  67.1 38.8 %copy-start.5 = (bf16[1024]{0:T(1024)(128)(2,1)S(1)}, bf16[1024]{0:T(1024)(128)(2,1)}, u32[]{:S(2)}) copy-start(bf16[1024]{0:T(1024)(128)(2,1)} %param.21) | copy-start | bytes 6148
  105.1 0.8 copy-start.3
  319.4 17.8 %all-to-all-start.3 = ((bf16[16,12,1024]{2,1,0:T(8,128)(2,1)}), bf16[16,12,1024]{2,1,0:T(8,128)(2,1)S(1)}, u32[]{:S(2)}, u32[]{:S(2)}) async-start(bf16[16,12,1024]{2,1,0:T(8,128)(2,1)} %reshape.143), calls=%async_computation.3 | async-start | bytes 1048576 | tf_op jit(solution)/shard_map/all_to_all | solution.py:104
Sparse Core Ops, SparseCore 0:
  105.2 73.0 all-gather.2
where the time goes:
time: 352 us; the launch traced here: 346 us
  waiting for transfers between devices  116 us (33%)
  matrix products  89.4 us (25%)
  local copies, waits for them, and re-layouts  75 us (21%)
  other arithmetic  32.9 us (9%)
  starting transfers between devices  18.1 us (5%)
  between operations  13.7 us (4%)
    all_gather x1, waiting for transfers between devices, entering(): everything = lax.all_gather(shard.astype(jnp.bfloat16), axis)  71.4 us
    dynamic_slice x32, local copies, waits for them, and re-layouts, turn(): new = combine(before, everything[k].astype(shard.dtype))  54.9 us
    dot_general x32, matrix products, feature_map(): projected = jnp.dot(rows, weight, preferred_element_type=jnp.float32)  40.3 us
    select_n x16, other arithmetic, turn(): return jnp.where(reached, new, before)  18.5 us
    dot_general x16, matrix products, query_section(): jnp.einsum('sf,tf->st', phi_query, phi_key, preferred_element_type=jnp.fl...  16 us
    dot_general x16, matrix products, query_section(): jnp.dot(scores, value_head.astype(jnp.float32), precision=lax.Precision.H...  15.8 us
    all_to_all x1, waiting for transfers between devices, per_device(): lax.all_to_all(returning, 'seq', split_axis=0, concat_axis=0, tiled=True)  14.1 us
    dot_general x16, matrix products, key_section(): jnp.einsum('tf,tv->fv', phi_key, value_head, preferred_element_type=jnp.f...  12.8 us
  transfers between devices with their start and end apart: 5, of which 5 were waited for; matrix products, arithmetic and copies ran while one was open for 2% of the time, Pallas kernels for 0%

commit v1 on v0

v1 whole, which is shorter than its diff:
```python
import functools

import jax
import jax.numpy as jnp
from jax import lax
from jax.experimental import pallas as pl
from jax.experimental.pallas import tpu as pltpu
from jax.sharding import PartitionSpec as P

MESH = pl.DeviceIdType.MESH
F32 = jnp.float32
BF16 = jnp.bfloat16


def kernel(
    n,
    heads,
    q_ref,
    k_ref,
    v_ref,
    w_ref,
    gain_ref,
    counts_ref,
    offsets_ref,
    out_ref,
    send,
    recv,
    phi_q,
    phi_kt,
    val,
    posr,
    post,
    posc,
    wq,
    wkt,
    out_send,
    out_recv,
    send_sem,
    recv_sem,
    back_send_sem,
    back_recv_sem,
):
    rows = q_ref.shape[0]
    half = rows // 2
    width = q_ref.shape[1] // heads
    feat = w_ref.shape[2]
    group = n // heads
    part_rows = rows // group
    part_half = part_rows // 2
    total = n * rows
    queries = n * part_rows
    me = lax.axis_index("seq")
    head = me // group
    part = me % group

    barrier = pltpu.get_barrier_semaphore()

    def greet(step, carry):
        peer = lax.rem(me + step, n)
        pl.semaphore_signal(barrier, inc=1, device_id={"seq": peer}, device_id_type=MESH)
        return carry

    lax.fori_loop(1, n, greet, 0)

    for pair in range(heads // 2):
        lanes = slice(2 * width * pair, 2 * width * (pair + 1))
        q = q_ref[:, lanes]
        k = k_ref[:, lanes]
        v = v_ref[:, lanes]
        send[2 * pair, 0:rows, :] = jnp.concatenate([q[:, :width], k[:, :width]], axis=1)
        send[2 * pair + 1, 0:rows, :] = jnp.concatenate([q[:, width:], k[:, width:]], axis=1)
        send[2 * pair, rows:, :] = jnp.concatenate([v[:half, :width], v[half:, :width]], axis=1)
        send[2 * pair + 1, rows:, :] = jnp.concatenate([v[:half, width:], v[half:, width:]], axis=1)

    pl.semaphore_wait(barrier, n - 1)

    def forward(peer):
        return pltpu.make_async_remote_copy(
            src_ref=send.at[peer // group],
            dst_ref=recv.at[me],
            send_sem=send_sem.at[peer],
            recv_sem=recv_sem.at[me],
            device_id={"seq": peer},
            device_id_type=MESH,
        )

    def send_one(step, carry):
        forward(lax.rem(me + step, n)).start()
        return carry

    lax.fori_loop(1, n, send_one, 0)
    recv[me] = send[head]

    lane = lax.broadcasted_iota(jnp.int32, (n, rows), 1)
    start = jnp.zeros((n, 1), jnp.int32)
    position = lane
    for d in range(n):
        count = counts_ref[:, d : d + 1]
        inside = (lane >= start) & (lane < start + count)
        position = position + jnp.where(inside, d * rows + offsets_ref[:, d : d + 1] - start, 0)
        start = start + count
    position = position.astype(F32)
    posr[...] = position
    if n < rows:
        position = jnp.concatenate([position, jnp.zeros((rows - n, rows), F32)], axis=0)
    post[...] = position.T
    mine = post[pl.ds(pl.multiple_of(part * part_rows, part_rows), part_rows), :]
    for j in range(n):
        posc[j * part_rows : (j + 1) * part_rows, :] = jnp.broadcast_to(
            mine[:, j : j + 1], (part_rows, 128)
        )

    w = w_ref[head]
    blank = jnp.zeros_like(w)
    wq[...] = jnp.concatenate([w, blank], axis=0)
    wkt[...] = jnp.concatenate([blank, w], axis=0).astype(F32).T.astype(BF16)
    gain = jnp.zeros((1, width), F32)
    for h in range(heads):
        gain = gain + jnp.where(head == h, gain_ref[:, h * width : (h + 1) * width].astype(F32), 0.0)

    def feature(z):
        return jnp.where(z > 0.0, z + 1.0, jnp.exp(jnp.minimum(z, 0.0))).astype(BF16)

    def take_block(src):
        x = recv[src, 0:rows, :]
        keys = lax.dot_general(wkt[...], x, (((1,), (1,)), ((), ())), preferred_element_type=F32)
        phi_kt[:, pl.ds(pl.multiple_of(src * rows, rows), rows)] = feature(keys)
        xq = recv[src, pl.ds(pl.multiple_of(part * part_rows, part_rows), part_rows), :]
        proj = jnp.dot(xq, wq[...], preferred_element_type=F32)
        phi_q[pl.ds(pl.multiple_of(src * part_rows, part_rows), part_rows), :] = feature(proj)
        block = recv[src, rows:, :]
        val[pl.ds(pl.multiple_of(src * rows, rows), half), :] = block[:, :width]
        val[pl.ds(pl.multiple_of(src * rows + half, half), half), :] = block[:, width:]

    take_block(me)

    def arrive(step, carry):
        src = lax.rem(me + n - step, n)
        pltpu.make_async_remote_copy(
            src_ref=send.at[0],
            dst_ref=recv.at[src],
            send_sem=send_sem.at[src],
            recv_sem=recv_sem.at[src],
            device_id={"seq": src},
            device_id_type=MESH,
        ).wait_recv()
        take_block(src)
        return carry

    lax.fori_loop(1, n, arrive, 0)

    tile_r = min(512, queries)
    tile_s = min(512, total)
    per_r = tile_r // part_rows
    per_s = tile_s // rows
    blocks = queries // tile_r

    def back(loader):
        return pltpu.make_async_remote_copy(
            src_ref=out_send.at[loader],
            dst_ref=out_recv.at[me],
            send_sem=back_send_sem.at[loader],
            recv_sem=back_recv_sem.at[me],
            device_id={"seq": loader},
            device_id_type=MESH,
        )

    def attend(step, carry):
        rb = lax.rem(me // per_r + step, blocks)
        r0 = pl.multiple_of(rb * tile_r, tile_r)
        fq = phi_q[pl.ds(r0, tile_r), :]
        pc = posc[pl.ds(r0, tile_r), :]
        pc = jnp.concatenate([pc] * per_s, axis=1)

        def over(sb, acc):
            s0 = pl.multiple_of(sb * tile_s, tile_s)
            scores = jnp.dot(fq, phi_kt[:, pl.ds(s0, tile_s)], preferred_element_type=F32)
            pr = jnp.concatenate([posr[pl.ds(sb * per_s + i, 1), :] for i in range(per_s)], axis=1)
            scores = jnp.where(pr <= pc, scores, 0.0)
            high = scores.astype(BF16)
            low = (scores - high.astype(F32)).astype(BF16)
            vals = val[pl.ds(s0, tile_s), :]
            return (
                acc
                + jnp.dot(high, vals, preferred_element_type=F32)
                + jnp.dot(low, vals, preferred_element_type=F32)
            )

        attended = lax.fori_loop(0, total // tile_s, over, jnp.zeros((tile_r, width), F32))
        centre = jnp.mean(attended, axis=1, keepdims=True)
        centred = attended - centre
        spread = jnp.mean(centred * centred, axis=1, keepdims=True)
        normed = (centred * lax.rsqrt(spread + 1e-05) * gain).astype(BF16)
        for i in range(per_r):
            y = normed[i * part_rows : (i + 1) * part_rows]
            loader = rb * per_r + i
            out_send[loader] = jnp.concatenate([y[:part_half], y[part_half:]], axis=1)

        for i in range(per_r):
            loader = rb * per_r + i

            @pl.when(loader != me)
            def _():
                back(loader).start()

        return carry

    lax.fori_loop(0, blocks, attend, 0)
    out_recv[me] = out_send[me]

    def finish(step, carry):
        src = lax.rem(me + n - step, n)
        pltpu.make_async_remote_copy(
            src_ref=out_send.at[src],
            dst_ref=out_recv.at[src],
            send_sem=back_send_sem.at[src],
            recv_sem=back_recv_sem.at[src],
            device_id={"seq": src},
            device_id_type=MESH,
        ).wait_recv()
        return carry

    lax.fori_loop(1, n, finish, 0)

    for piece in range(group):
        first = slice(piece * part_rows, piece * part_rows + part_half)
        second = slice(piece * part_rows + part_half, (piece + 1) * part_rows)
        for pair in range(heads // 2):
            lanes = slice(2 * width * pair, 2 * width * (pair + 1))
            a = out_recv[2 * pair * group + piece]
            b = out_recv[(2 * pair + 1) * group + piece]
            out_ref[first, lanes] = jnp.concatenate([a[:, :width], b[:, :width]], axis=1)
            out_ref[second, lanes] = jnp.concatenate([a[:, width:], b[:, width:]], axis=1)

    def drain(step, carry):
        peer = lax.rem(me + step, n)
        forward(peer).wait_send()
        back(peer).wait_send()
        return carry

    lax.fori_loop(1, n, drain, 0)


def per_device(n, queries, keys, values, feat_weight, norm_gain, counts, offsets):
    rows = queries.shape[0]
    heads, width, feat = feat_weight.shape
    group = n // heads
    part_rows = rows // group
    total = n * rows
    lanes = 2 * width
    return pl.pallas_call(
        functools.partial(kernel, n, heads),
        out_shape=jax.ShapeDtypeStruct(queries.shape, BF16),
        in_specs=[pl.BlockSpec(memory_space=pltpu.VMEM)] * 7,
        out_specs=pl.BlockSpec(memory_space=pltpu.VMEM),
        scratch_shapes=[
            pltpu.VMEM((heads, rows + rows // 2, lanes), BF16),
            pltpu.VMEM((n, rows + rows // 2, lanes), BF16),
            pltpu.VMEM((n * part_rows, feat), BF16),
            pltpu.VMEM((feat, total), BF16),
            pltpu.VMEM((total, width), BF16),
            pltpu.VMEM((n, rows), F32),
            pltpu.VMEM((rows, max(n, rows)), F32),
            pltpu.VMEM((n * part_rows, 128), F32),
            pltpu.VMEM((lanes, feat), BF16),
            pltpu.VMEM((feat, lanes), BF16),
            pltpu.VMEM((n, part_rows // 2, lanes), BF16),
            pltpu.VMEM((n, part_rows // 2, lanes), BF16),
            pltpu.SemaphoreType.DMA((n,)),
            pltpu.SemaphoreType.DMA((n,)),
            pltpu.SemaphoreType.DMA((n,)),
            pltpu.SemaphoreType.DMA((n,)),
        ],
        compiler_params=pltpu.CompilerParams(
            collective_id=0, has_side_effects=True, vmem_limit_bytes=48 * 1024 * 1024
        ),
    )(queries, keys, values, feat_weight, norm_gain.reshape(1, -1), counts, offsets)


def solution(mesh):
    in_specs = (
        P(("dp", "seq"), None),
        P(("dp", "seq"), None),
        P(("dp", "seq"), None),
        P(),
        P(),
        P("dp", None),
        P("dp", None),
    )
    return jax.shard_map(
        functools.partial(per_device, mesh.shape["seq"]),
        mesh=mesh,
        in_specs=in_specs,
        out_specs=P(("dp", "seq"), None),
        check_vma=False,
    )
```

time: 352 us -> 49.7 us (0.14); the launches traced: 346 us -> 49.4 us
  waiting for transfers between devices: 116 us -> 0 us
  matrix products: 89.4 us -> 0 us
  local copies, waits for them, and re-layouts: 75 us -> 6.67 us
  Pallas kernels: 0 us -> 42.7 us
  other arithmetic: 32.9 us -> 0 us
  starting transfers between devices: 18.1 us -> 0 us
  between operations: 13.7 us -> 0.02 us
    dot_general x96 -> x0, matrix products: 89.4 us -> none  [the longest x32 40.3 us: feature_map(): projected = jnp.dot(rows, weight, preferred_element_type=jnp.float32)]
    all_gather x1 -> x0, waiting for transfers between devices: 71.4 us -> none  [entering(): everything = lax.all_gather(shard.astype(jnp.bfloat16), axis)]
    dynamic_slice x34 -> x0, local copies, waits for them, and re-layouts: 56 us -> none  [the longest x32 54.9 us: turn(): new = combine(before, everything[k].astype(shard.dtype))]
    all_to_all x4 -> x0, waiting for transfers between devices: 44.1 us -> none  [the longest x1 14.1 us: per_device(): lax.all_to_all(returning, 'seq', split_axis=0, concat_axis=0, tiled=True)]
    pallas_call x0 -> x1, Pallas kernels: none -> 42.7 us  [per_device(): pl.pallas_call(functools.partial(kernel, n, heads), out_shape=jax.ShapeDt...]
    select_n x21 -> x0, other arithmetic: 19.5 us -> none  [the longest x16 18.5 us: turn(): return jnp.where(reached, new, before)]
    all_to_all x4 -> x0, starting transfers between devices: 18.1 us -> none  [the longest x1 7.41 us: per_device(): lax.all_to_all(out_key, 'seq', split_axis=0, concat_axis=0, tiled=True)]
    dynamic_update_slice x16 -> x0, other arithmetic: 11 us -> none  [per_device(): lax.map(query_section, (query_heads, phi_keys, value_heads, feat_weight,...]
  transfers between devices with their start and end apart: 5 -> 0, of which waited for: 5 -> 0; matrix products, arithmetic and copies ran while one was open for 2% -> 0% of each run, Pallas kernels for 0% -> 0%
where the time goes in v1:
time: 49.7 us; the launch traced here: 49.4 us
  Pallas kernels  42.7 us (86%)
  local copies, waits for them, and re-layouts  6.67 us (13%)
    pallas_call x1, Pallas kernels, per_device(): pl.pallas_call(functools.partial(kernel, n, heads), out_shape=jax.ShapeDt...  42.7 us
    unnamed x13, local copies, waits for them, and re-layouts  5.99 us

profile of v1, /device:TPU:0, one launch (start us, length us, event | category | flops | bytes accessed | tf_op | source)
XLA Modules:
  0.0 49.4 jit_solution(5700489901012621382)
XLA Ops:
  0.0 0.7 %reshape.3.gain_ref = bf16[1,1024]{1,0:T(2,128)(2,1)S(1)} reshape(bf16[1024]{0:T(1024)(128)(2,1)} %param.11) | data formatting | bytes 4096 | tf_op jit(solution)/shard_map/reshape | solution.py:277
  0.7 0.0 copy-start
  0.7 1.0 %copy-done = bf16[16,64,256]{2,1,0:T(8,128)(2,1)S(1)} copy-done((bf16[16,64,256]{2,1,0:T(8,128)(2,1)S(1)}, bf16[16,64,256]{2,1,0:T(8,128)(2,1)}, u32[]{:S(2)}) %copy-start) | copy-done | bytes 524312
  1.7 0.0 copy-start.1
  1.7 0.9 %copy-done.1 = bf16[128,1024]{1,0:T(8,128)(2,1)S(1)} copy-done((bf16[128,1024]{1,0:T(8,128)(2,1)S(1)}, bf16[128,1024]{1,0:T(8,128)(2,1)}, u32[]{:S(2)}) %copy-start.1) | copy-done | bytes 262168
  2.7 0.0 copy-start.2
  2.7 0.9 %copy-done.2 = bf16[128,1024]{1,0:T(8,128)(2,1)S(1)} copy-done((bf16[128,1024]{1,0:T(8,128)(2,1)S(1)}, bf16[128,1024]{1,0:T(8,128)(2,1)}, u32[]{:S(2)}) %copy-start.2) | copy-done | bytes 262168
  3.6 0.0 copy-start.3
  3.6 0.9 %copy-done.3 = bf16[128,1024]{1,0:T(8,128)(2,1)S(1)} copy-done((bf16[128,1024]{1,0:T(8,128)(2,1)S(1)}, bf16[128,1024]{1,0:T(8,128)(2,1)}, u32[]{:S(2)}) %copy-start.3) | copy-done | bytes 262168
  4.6 0.0 copy-start.4
  4.6 0.7 %copy-done.4 = s32[16,16]{1,0:T(8,128)S(1)} copy-done((s32[16,16]{1,0:T(8,128)S(1)}, s32[16,16]{1,0:T(8,128)}, u32[]{:S(2)}) %copy-start.4) | copy-done | bytes 1048
  5.3 0.0 copy-start.5
  5.3 0.7 %copy-done.5 = s32[16,16]{1,0:T(8,128)S(1)} copy-done((s32[16,16]{1,0:T(8,128)S(1)}, s32[16,16]{1,0:T(8,128)}, u32[]{:S(2)}) %copy-start.5) | copy-done | bytes 1048
  6.0 42.7 %shard_map.73 = bf16[128,1024]{1,0:T(8,128)(2,1)S(1)} custom-call(bf16[128,1024]{1,0:T(8,128)(2,1)S(1)} %copy-done.1, bf16[128,1024]{1,0:T(8,128)(2,1)S(1)} %copy-done.2, bf16[128,1024]{1,0:T(8,128)(2,1)S(1)} %copy-done.3, bf16[16,64,256]{2,1,0:T(8,128)(2,1)S(1)} %copy-done, bf16[1,1024]{1,0:T(2,128)(2,1)S(1)} %reshape.3.gain_ref, s32[16,16]{1,0:T(8,128)S(1)} %copy-done.4, ...), custom_call_target="tpu_custom_call" | custom-call | tf_op jit(solution)/shard_map/pallas_call | solution.py:251
  48.7 0.7 %copy.9 = bf16[128,1024]{1,0:T(8,128)(2,1)} copy(bf16[128,1024]{1,0:T(8,128)(2,1)S(1)} %shard_map.73) | data formatting | bytes 524288
Async XLA Ops:
  0.7 1.0 %copy-start = (bf16[16,64,256]{2,1,0:T(8,128)(2,1)S(1)}, bf16[16,64,256]{2,1,0:T(8,128)(2,1)}, u32[]{:S(2)}) copy-start(bf16[16,64,256]{2,1,0:T(8,128)(2,1)} %w_ref.1) | copy-start | bytes 1572868
  1.7 0.9 %copy-start.1 = (bf16[128,1024]{1,0:T(8,128)(2,1)S(1)}, bf16[128,1024]{1,0:T(8,128)(2,1)}, u32[]{:S(2)}) copy-start(bf16[128,1024]{1,0:T(8,128)(2,1)} %q_ref.1) | copy-start | bytes 786436
  2.7 0.9 %copy-start.2 = (bf16[128,1024]{1,0:T(8,128)(2,1)S(1)}, bf16[128,1024]{1,0:T(8,128)(2,1)}, u32[]{:S(2)}) copy-start(bf16[128,1024]{1,0:T(8,128)(2,1)} %k_ref.1) | copy-start | bytes 786436
  3.6 0.9 %copy-start.3 = (bf16[128,1024]{1,0:T(8,128)(2,1)S(1)}, bf16[128,1024]{1,0:T(8,128)(2,1)}, u32[]{:S(2)}) copy-start(bf16[128,1024]{1,0:T(8,128)(2,1)} %v_ref.1) | copy-start | bytes 786436
  4.6 0.7 %copy-start.4 = (s32[16,16]{1,0:T(8,128)S(1)}, s32[16,16]{1,0:T(8,128)}, u32[]{:S(2)}) copy-start(s32[16,16]{1,0:T(8,128)} %counts_ref.1) | copy-start | bytes 3076
  5.3 0.7 %copy-start.5 = (s32[16,16]{1,0:T(8,128)S(1)}, s32[16,16]{1,0:T(8,128)}, u32[]{:S(2)}) copy-start(s32[16,16]{1,0:T(8,128)} %offsets_ref.1) | copy-start | bytes 3076

commit v2 on v1

v2 whole, which is shorter than its diff:
```python
import functools

import jax
import jax.numpy as jnp
from jax import lax
from jax.experimental import pallas as pl
from jax.experimental.pallas import tpu as pltpu
from jax.sharding import PartitionSpec as P

MESH = pl.DeviceIdType.MESH
F32 = jnp.float32
BF16 = jnp.bfloat16
GROUPS = 4


def kernel(
    n,
    heads,
    q_ref,
    k_ref,
    v_ref,
    w_ref,
    gain_ref,
    counts_ref,
    offsets_ref,
    out_ref,
    q_buf,
    k_buf,
    v_buf,
    w_buf,
    gain_buf,
    counts_buf,
    offsets_buf,
    load_sem,
    send,
    recv,
    phi_q,
    phi_kt,
    val,
    posr,
    post,
    posc,
    slot_row,
    slot_col,
    acc,
    wq,
    wkt,
    out_send,
    out_recv,
    send_sem,
    recv_sem,
    back_send_sem,
    back_recv_sem,
):
    rows = q_ref.shape[0]
    half = rows // 2
    width = q_ref.shape[1] // heads
    feat = w_ref.shape[2]
    group = n // heads
    part_rows = rows // group
    part_half = part_rows // 2
    total = n * rows
    queries = n * part_rows
    me = lax.axis_index("seq")
    head = me // group
    part = me % group

    half_ring = n // 2
    own = me // half_ring * half_ring
    other = lax.rem(own + half_ring, n)

    def target(step):
        return jnp.where(step < half_ring, own, other) + lax.rem(me + step, half_ring)

    def source(step):
        return jnp.where(step < half_ring, own, other) + lax.rem(me + n - step, half_ring)

    loads = [
        pltpu.make_async_copy(src, dst, load_sem.at[i])
        for i, (src, dst) in enumerate(
            (
                (q_ref, q_buf),
                (k_ref, k_buf),
                (v_ref, v_buf),
                (counts_ref, counts_buf),
                (offsets_ref, offsets_buf),
                (w_ref.at[head], w_buf),
                (gain_ref, gain_buf),
            )
        )
    ]
    for load in loads:
        load.start()

    barrier = pltpu.get_barrier_semaphore()

    def greet(step, carry):
        peer = lax.rem(me + step, n)
        pl.semaphore_signal(barrier, inc=1, device_id={"seq": peer}, device_id_type=MESH)
        return carry

    lax.fori_loop(1, n, greet, 0)

    for load in loads[:3]:
        load.wait()

    for pair in range(heads // 2):
        lanes = slice(2 * width * pair, 2 * width * (pair + 1))
        q = q_buf[:, lanes]
        k = k_buf[:, lanes]
        v = v_buf[:, lanes]
        send[2 * pair, 0:rows, :] = jnp.concatenate([q[:, :width], k[:, :width]], axis=1)
        send[2 * pair + 1, 0:rows, :] = jnp.concatenate([q[:, width:], k[:, width:]], axis=1)
        send[2 * pair, rows:, :] = jnp.concatenate([v[:half, :width], v[half:, :width]], axis=1)
        send[2 * pair + 1, rows:, :] = jnp.concatenate([v[:half, width:], v[half:, width:]], axis=1)

    pl.semaphore_wait(barrier, n - 1)

    def forward(peer):
        return pltpu.make_async_remote_copy(
            src_ref=send.at[peer // group],
            dst_ref=recv.at[me],
            send_sem=send_sem.at[peer],
            recv_sem=recv_sem.at[me],
            device_id={"seq": peer},
            device_id_type=MESH,
        )

    def send_one(step, carry):
        forward(target(step)).start()
        return carry

    lax.fori_loop(1, n, send_one, 0)
    recv[me] = send[head]

    for load in loads[3:]:
        load.wait()

    lane = lax.broadcasted_iota(jnp.int32, (n, rows), 1)
    start = jnp.zeros((n, 1), jnp.int32)
    position = lane
    for d in range(n):
        count = counts_buf[:, d : d + 1]
        inside = (lane >= start) & (lane < start + count)
        position = position + jnp.where(inside, d * rows + offsets_buf[:, d : d + 1] - start, 0)
        start = start + count
    position = position.astype(F32)
    posr[...] = position
    if n < rows:
        position = jnp.concatenate([position, jnp.zeros((rows - n, rows), F32)], axis=0)
    post[...] = position.T
    mine = post[pl.ds(pl.multiple_of(part * part_rows, part_rows), part_rows), :]
    for j in range(n):
        posc[j * part_rows : (j + 1) * part_rows, :] = jnp.broadcast_to(
            mine[:, j : j + 1], (part_rows, 128)
        )

    w = w_buf[...]
    blank = jnp.zeros_like(w)
    wq[...] = jnp.concatenate([w, blank], axis=0)
    wkt[...] = jnp.concatenate([blank, w], axis=0).astype(F32).T.astype(BF16)
    gain = jnp.zeros((1, width), F32)
    for h in range(heads):
        gain = gain + jnp.where(head == h, gain_buf[:, h * width : (h + 1) * width].astype(F32), 0.0)

    def feature(z):
        return jnp.where(z > 0.0, z + 1.0, jnp.exp(jnp.minimum(z, 0.0))).astype(BF16)

    def take_block(step):
        src = source(step)
        x = recv[src, 0:rows, :]
        keys = lax.dot_general(wkt[...], x, (((1,), (1,)), ((), ())), preferred_element_type=F32)
        phi_kt[:, step * rows : (step + 1) * rows] = feature(keys)
        mine_of = pl.multiple_of(part * part_rows, part_rows)
        proj = jnp.dot(
            recv[src, pl.ds(mine_of, part_rows), :], wq[...], preferred_element_type=F32
        )
        slots = slice(step * part_rows, (step + 1) * part_rows)
        phi_q[slots, :] = feature(proj)
        block = recv[src, rows:, :]
        val[step * rows : step * rows + half, :] = block[:, :width]
        val[step * rows + half : (step + 1) * rows, :] = block[:, width:]
        slot_row[step : step + 1, :] = posr[pl.ds(src, 1), :]
        slot_col[slots, :] = posc[
            pl.ds(pl.multiple_of(src * part_rows, part_rows), part_rows), :
        ]

    def arrive(step):
        src = source(step)
        pltpu.make_async_remote_copy(
            src_ref=send.at[0],
            dst_ref=recv.at[src],
            send_sem=send_sem.at[src],
            recv_sem=recv_sem.at[src],
            device_id={"seq": src},
            device_id_type=MESH,
        ).wait_recv()

    groups = min(GROUPS, n)
    per = n // groups
    tile_r = per * part_rows
    tile_s = per * rows

    def tile(rb, sb):
        r0 = pl.multiple_of(rb * tile_r, tile_r)
        s0 = pl.multiple_of(sb * tile_s, tile_s)
        scores = jnp.dot(
            phi_q[pl.ds(r0, tile_r), :], phi_kt[:, pl.ds(s0, tile_s)], preferred_element_type=F32
        )
        later = jnp.concatenate([slot_col[pl.ds(r0, tile_r), :]] * per, axis=1)
        earlier = jnp.concatenate([slot_row[pl.ds(sb * per + i, 1), :] for i in range(per)], axis=1)
        scores = jnp.where(earlier <= later, scores, 0.0)
        high = scores.astype(BF16)
        low = (scores - high.astype(F32)).astype(BF16)
        vals = val[pl.ds(s0, tile_s), :]
        return jnp.dot(high, vals, preferred_element_type=F32) + jnp.dot(
            low, vals, preferred_element_type=F32
        )

    def back(step):
        loader = source(step)
        return pltpu.make_async_remote_copy(
            src_ref=out_send.at[step],
            dst_ref=out_recv.at[me],
            send_sem=back_send_sem.at[loader],
            recv_sem=back_recv_sem.at[me],
            device_id={"seq": loader},
            device_id_type=MESH,
        )

    def finish(rb, attended):
        centre = jnp.mean(attended, axis=1, keepdims=True)
        centred = attended - centre
        spread = jnp.mean(centred * centred, axis=1, keepdims=True)
        normed = (centred * lax.rsqrt(spread + 1e-05) * gain).astype(BF16)
        for i in range(per):
            y = normed[i * part_rows : (i + 1) * part_rows]
            out_send[rb * per + i] = jnp.concatenate([y[:part_half], y[part_half:]], axis=1)
        for i in range(per):
            if rb * per + i > 0:
                back(rb * per + i).start()

    def rows_of(rb):
        return pl.ds(pl.multiple_of(rb * tile_r, tile_r), tile_r)

    for gi in range(groups):
        for step in range(gi * per, (gi + 1) * per):
            if step > 0:
                arrive(step)
            take_block(step)
        last = gi == groups - 1
        fresh = tile(gi, gi)
        if not last:

            def both(i, fresh):
                acc[rows_of(i), :] = acc[rows_of(i), :] + tile(i, gi)
                return fresh + tile(gi, i)

            acc[rows_of(gi), :] = lax.fori_loop(0, gi, both, fresh)
        else:
            finish(gi, lax.fori_loop(0, gi, lambda i, fresh: fresh + tile(gi, i), fresh))
            for i in reversed(range(gi)):
                finish(i, acc[rows_of(i), :] + tile(i, gi))
    out_recv[me] = out_send[0]

    def collect(step, carry):
        src = source(step)
        pltpu.make_async_remote_copy(
            src_ref=out_send.at[step],
            dst_ref=out_recv.at[src],
            send_sem=back_send_sem.at[src],
            recv_sem=back_recv_sem.at[src],
            device_id={"seq": src},
            device_id_type=MESH,
        ).wait_recv()
        return carry

    lax.fori_loop(1, n, collect, 0)

    for piece in range(group):
        first = slice(piece * part_rows, piece * part_rows + part_half)
        second = slice(piece * part_rows + part_half, (piece + 1) * part_rows)
        for pair in range(heads // 2):
            lanes = slice(2 * width * pair, 2 * width * (pair + 1))
            a = out_recv[2 * pair * group + piece]
            b = out_recv[(2 * pair + 1) * group + piece]
            out_ref[first, lanes] = jnp.concatenate([a[:, :width], b[:, :width]], axis=1)
            out_ref[second, lanes] = jnp.concatenate([a[:, width:], b[:, width:]], axis=1)

    def drain(step, carry):
        peer = target(step)
        forward(peer).wait_send()
        back(step).wait_send()
        return carry

    lax.fori_loop(1, n, drain, 0)


def per_device(n, queries, keys, values, feat_weight, norm_gain, counts, offsets):
    rows = queries.shape[0]
    heads, width, feat = feat_weight.shape
    group = n // heads
    part_rows = rows // group
    total = n * rows
    lanes = 2 * width
    return pl.pallas_call(
        functools.partial(kernel, n, heads),
        out_shape=jax.ShapeDtypeStruct(queries.shape, BF16),
        in_specs=[pl.BlockSpec(memory_space=pltpu.HBM)] * 7,
        out_specs=pl.BlockSpec(memory_space=pltpu.VMEM),
        scratch_shapes=[
            pltpu.VMEM(queries.shape, BF16),
            pltpu.VMEM(keys.shape, BF16),
            pltpu.VMEM(values.shape, BF16),
            pltpu.VMEM((width, feat), BF16),
            pltpu.VMEM((1, norm_gain.shape[0]), BF16),
            pltpu.VMEM(counts.shape, jnp.int32),
            pltpu.VMEM(offsets.shape, jnp.int32),
            pltpu.SemaphoreType.DMA((7,)),
            pltpu.VMEM((heads, rows + rows // 2, lanes), BF16),
            pltpu.VMEM((n, rows + rows // 2, lanes), BF16),
            pltpu.VMEM((n * part_rows, feat), BF16),
            pltpu.VMEM((feat, total), BF16),
            pltpu.VMEM((total, width), BF16),
            pltpu.VMEM((n, rows), F32),
            pltpu.VMEM((rows, max(n, rows)), F32),
            pltpu.VMEM((n * part_rows, 128), F32),
            pltpu.VMEM((n, rows), F32),
            pltpu.VMEM((n * part_rows, 128), F32),
            pltpu.VMEM((n * part_rows, width), F32),
            pltpu.VMEM((lanes, feat), BF16),
            pltpu.VMEM((feat, lanes), BF16),
            pltpu.VMEM((n, part_rows // 2, lanes), BF16),
            pltpu.VMEM((n, part_rows // 2, lanes), BF16),
            pltpu.SemaphoreType.DMA((n,)),
            pltpu.SemaphoreType.DMA((n,)),
            pltpu.SemaphoreType.DMA((n,)),
            pltpu.SemaphoreType.DMA((n,)),
        ],
        compiler_params=pltpu.CompilerParams(
            collective_id=0, has_side_effects=True, vmem_limit_bytes=48 * 1024 * 1024
        ),
    )(queries, keys, values, feat_weight, norm_gain.reshape(1, -1), counts, offsets)


def solution(mesh):
    in_specs = (
        P(("dp", "seq"), None),
        P(("dp", "seq"), None),
        P(("dp", "seq"), None),
        P(),
        P(),
        P("dp", None),
        P("dp", None),
    )
    return jax.shard_map(
        functools.partial(per_device, mesh.shape["seq"]),
        mesh=mesh,
        in_specs=in_specs,
        out_specs=P(("dp", "seq"), None),
        check_vma=False,
    )
```

time: 49.7 us -> 43 us (0.87)
  Pallas kernels: 42.7 us -> 36 us
    pallas_call x1, Pallas kernels: 42.7 us -> 36 us  [per_device(): pl.pallas_call(functools.partial(kernel, n, heads), out_shape=jax.ShapeDt...]
where the time goes in v2:
time: 43 us; the launch traced here: 42.7 us
  Pallas kernels  36 us (84%)
  local copies, waits for them, and re-layouts  6.67 us (16%)
    pallas_call x1, Pallas kernels, per_device(): pl.pallas_call(functools.partial(kernel, n, heads), out_shape=jax.ShapeDt...  36 us
    unnamed x13, local copies, waits for them, and re-layouts  5.99 us

profile of v2, /device:TPU:0, one launch (start us, length us, event | category | flops | bytes accessed | tf_op | source)
XLA Modules:
  0.0 42.7 jit_solution(6791570758576909778)
XLA Ops:
  0.0 0.7 %reshape.3.gain_ref = bf16[1,1024]{1,0:T(2,128)(2,1)S(1)} reshape(bf16[1024]{0:T(1024)(128)(2,1)} %param.11) | data formatting | bytes 4096 | tf_op jit(solution)/shard_map/reshape | solution.py:343
  0.7 0.0 copy-start
  0.7 1.0 %copy-done = bf16[16,64,256]{2,1,0:T(8,128)(2,1)S(1)} copy-done((bf16[16,64,256]{2,1,0:T(8,128)(2,1)S(1)}, bf16[16,64,256]{2,1,0:T(8,128)(2,1)}, u32[]{:S(2)}) %copy-start) | copy-done | bytes 524312
  1.7 0.0 copy-start.1
  1.7 0.9 %copy-done.1 = bf16[128,1024]{1,0:T(8,128)(2,1)S(1)} copy-done((bf16[128,1024]{1,0:T(8,128)(2,1)S(1)}, bf16[128,1024]{1,0:T(8,128)(2,1)}, u32[]{:S(2)}) %copy-start.1) | copy-done | bytes 262168
  2.7 0.0 copy-start.2
  2.7 0.9 %copy-done.2 = bf16[128,1024]{1,0:T(8,128)(2,1)S(1)} copy-done((bf16[128,1024]{1,0:T(8,128)(2,1)S(1)}, bf16[128,1024]{1,0:T(8,128)(2,1)}, u32[]{:S(2)}) %copy-start.2) | copy-done | bytes 262168
  3.6 0.0 copy-start.3
  3.6 0.9 %copy-done.3 = bf16[128,1024]{1,0:T(8,128)(2,1)S(1)} copy-done((bf16[128,1024]{1,0:T(8,128)(2,1)S(1)}, bf16[128,1024]{1,0:T(8,128)(2,1)}, u32[]{:S(2)}) %copy-start.3) | copy-done | bytes 262168
  4.6 0.0 copy-start.4
  4.6 0.7 %copy-done.4 = s32[16,16]{1,0:T(8,128)S(1)} copy-done((s32[16,16]{1,0:T(8,128)S(1)}, s32[16,16]{1,0:T(8,128)}, u32[]{:S(2)}) %copy-start.4) | copy-done | bytes 1048
  5.3 0.0 copy-start.5
  5.3 0.7 %copy-done.5 = s32[16,16]{1,0:T(8,128)S(1)} copy-done((s32[16,16]{1,0:T(8,128)S(1)}, s32[16,16]{1,0:T(8,128)}, u32[]{:S(2)}) %copy-start.5) | copy-done | bytes 1048
  6.0 36.0 %shard_map.73 = bf16[128,1024]{1,0:T(8,128)(2,1)S(1)} custom-call(bf16[128,1024]{1,0:T(8,128)(2,1)S(1)} %copy-done.1, bf16[128,1024]{1,0:T(8,128)(2,1)S(1)} %copy-done.2, bf16[128,1024]{1,0:T(8,128)(2,1)S(1)} %copy-done.3, bf16[16,64,256]{2,1,0:T(8,128)(2,1)S(1)} %copy-done, bf16[1,1024]{1,0:T(2,128)(2,1)S(1)} %reshape.3.gain_ref, s32[16,16]{1,0:T(8,128)S(1)} %copy-done.4, ...), custom_call_target="tpu_custom_call" | custom-call | tf_op jit(solution)/shard_map/pallas_call | solution.py:306
  42.0 0.7 %copy.9 = bf16[128,1024]{1,0:T(8,128)(2,1)} copy(bf16[128,1024]{1,0:T(8,128)(2,1)S(1)} %shard_map.73) | data formatting | bytes 524288
Async XLA Ops:
  0.7 1.0 %copy-start = (bf16[16,64,256]{2,1,0:T(8,128)(2,1)S(1)}, bf16[16,64,256]{2,1,0:T(8,128)(2,1)}, u32[]{:S(2)}) copy-start(bf16[16,64,256]{2,1,0:T(8,128)(2,1)} %w_ref.1) | copy-start | bytes 1572868
  1.7 0.9 %copy-start.1 = (bf16[128,1024]{1,0:T(8,128)(2,1)S(1)}, bf16[128,1024]{1,0:T(8,128)(2,1)}, u32[]{:S(2)}) copy-start(bf16[128,1024]{1,0:T(8,128)(2,1)} %q_ref.1) | copy-start | bytes 786436
  2.7 0.9 %copy-start.2 = (bf16[128,1024]{1,0:T(8,128)(2,1)S(1)}, bf16[128,1024]{1,0:T(8,128)(2,1)}, u32[]{:S(2)}) copy-start(bf16[128,1024]{1,0:T(8,128)(2,1)} %k_ref.1) | copy-start | bytes 786436
  3.6 0.9 %copy-start.3 = (bf16[128,1024]{1,0:T(8,128)(2,1)S(1)}, bf16[128,1024]{1,0:T(8,128)(2,1)}, u32[]{:S(2)}) copy-start(bf16[128,1024]{1,0:T(8,128)(2,1)} %v_ref.1) | copy-start | bytes 786436
  4.6 0.7 %copy-start.4 = (s32[16,16]{1,0:T(8,128)S(1)}, s32[16,16]{1,0:T(8,128)}, u32[]{:S(2)}) copy-start(s32[16,16]{1,0:T(8,128)} %counts_ref.1) | copy-start | bytes 3076
  5.3 0.7 %copy-start.5 = (s32[16,16]{1,0:T(8,128)S(1)}, s32[16,16]{1,0:T(8,128)}, u32[]{:S(2)}) copy-start(s32[16,16]{1,0:T(8,128)} %offsets_ref.1) | copy-start | bytes 3076

commit v3 on v2

--- a/solution.py
+++ b/solution.py
@@ -338,7 +338,7 @@
             pltpu.SemaphoreType.DMA((n,)),
         ],
         compiler_params=pltpu.CompilerParams(
-            collective_id=0, has_side_effects=True, vmem_limit_bytes=48 * 1024 * 1024
+            collective_id=0, has_side_effects=True, vmem_limit_bytes=67043328
         ),
     )(queries, keys, values, feat_weight, norm_gain.reshape(1, -1), counts, offsets)
 

time: 43 us -> 39.6 us (0.921)
  local copies, waits for them, and re-layouts: 6.67 us -> 2.95 us
  Pallas kernels: 36 us -> 36.5 us
    unnamed x13 -> x1, local copies, waits for them, and re-layouts: 5.99 us -> 1.67 us
    reshape x1, local copies, waits for them, and re-layouts: 0.69 us -> 1.28 us  [per_device(): norm_gain.reshape(1, -1)]
    pallas_call x1, Pallas kernels: 36 us -> 36.5 us  [per_device(): pl.pallas_call(functools.partial(kernel, n, heads), out_shape=jax.ShapeDt...]
where the time goes in v3:
time: 39.6 us; the launch traced here: 39.4 us
  Pallas kernels  36.5 us (92%)
  local copies, waits for them, and re-layouts  2.95 us (7%)
    pallas_call x1, Pallas kernels, per_device(): pl.pallas_call(functools.partial(kernel, n, heads), out_shape=jax.ShapeDt...  36.5 us
    unnamed x1, local copies, waits for them, and re-layouts  1.67 us
    reshape x1, local copies, waits for them, and re-layouts, per_device(): norm_gain.reshape(1, -1)  1.28 us

profile of v3, /device:TPU:0, one launch (start us, length us, event | category | flops | bytes accessed | tf_op | source)
XLA Modules:
  0.0 39.4 jit_solution(16823842896328260929)
XLA Ops:
  0.0 1.3 %reshape.3.gain_ref = bf16[1,1024]{1,0:T(2,128)(2,1)} reshape(bf16[1024]{0:T(1024)(128)(2,1)} %param.11) | data formatting | bytes 4096 | tf_op jit(solution)/shard_map/reshape | solution.py:343
  1.3 36.5 %shard_map.73 = bf16[128,1024]{1,0:T(8,128)(2,1)} custom-call(bf16[128,1024]{1,0:T(8,128)(2,1)} %q_ref.1, bf16[128,1024]{1,0:T(8,128)(2,1)} %k_ref.1, bf16[128,1024]{1,0:T(8,128)(2,1)} %v_ref.1, bf16[16,64,256]{2,1,0:T(8,128)(2,1)} %w_ref.1, bf16[1,1024]{1,0:T(2,128)(2,1)} %reshape.3.gain_ref, s32[16,16]{1,0:T(8,128)} %counts_ref.1, s32[16,16]{1,0:T(8,128)} %offsets_ref.1), custom_call_target="tpu_custom_call" | custom-call | tf_op jit(solution)/shard_map/pallas_call | solution.py:306
  37.7 1.7 %copy.9 = bf16[128,1024]{1,0:T(8,128)(2,1)} copy(bf16[128,1024]{1,0:T(8,128)(2,1)} %shard_map.73) | data formatting | bytes 524288
